TPU v7x, 256 devices: a whole 4x4x8 slice. The times are simulated.
256 devices in a mesh: grp: 4 (over x), tile: 64 (over z, y, core).
Axes of the slice: x: 4, y: 4, z: 8, core: 2. Of those that a mesh axis runs over, the one named last changes fastest.
Arguments:
- bricks: float32 [512, 128, 512], P(('grp', 'tile')), may hold values from 0 to 1
- colour_table: float32 [3, 256], replicated, may hold values from 0.5 to 8
- opacity_table: float32 [256], replicated, may hold values from 2e-05 to 0.005
- depth_order: int32 [4, 64], replicated, may hold values from 0 to 63, each once within a row
Outputs:
- image: float32 [4, 65536], P(None, ('grp', 'tile'))
Inputs may be any that keep to these rules, and one draw needn't show every extreme that they name: Each row of depth_order holds every number 0 .. 63 once.
All inputs are finite; a program needn't handle non-finite values.
Results may differ from a plain program's by a relative error of at most 0.0003.
Values sent between devices are 32-bit elements; how exact they have to be, the bound alone decides.
A program may use at most 64 MiB of HBM per device.

v0:
```python
import jax
import jax.numpy as jnp
from jax import lax
from jax.sharding import PartitionSpec as P


def shade_cells(values, palette):
    knot_count = palette.shape[1]
    position = values * (knot_count - 1)
    knot_pos = lax.broadcasted_iota(jnp.float32, (knot_count, 1), 0)
    weights = jnp.maximum(0.0, 1.0 - jnp.abs(position[None, :] - knot_pos))
    return jnp.dot(
        palette, weights, precision=lax.Precision.HIGHEST, preferred_element_type=jnp.float32
    )


def render(bricks, palette):
    depth_count = bricks.shape[0]
    pixels = bricks.shape[1] * bricks.shape[2]
    slices = bricks.reshape(depth_count, pixels)
    block_len = pixels // 8

    def one_slice(depth_at, carry):
        colour, transmit = carry
        values = lax.dynamic_index_in_dim(slices, depth_at, 0, keepdims=False)
        shaded = [
            shade_cells(lax.slice_in_dim(values, j * block_len, (j + 1) * block_len), palette)
            for j in range(8)
        ]
        sample = jnp.concatenate(shaded, axis=1)
        weight = transmit * sample[3]
        colour = colour + weight[None, :] * sample[:3]
        transmit = transmit * (1.0 - sample[3])
        return (colour, transmit)

    start = (jnp.zeros((3, pixels), jnp.float32), jnp.ones((pixels,), jnp.float32))
    colour, transmit = lax.fori_loop(0, depth_count, one_slice, start)
    return jnp.concatenate([colour, (1.0 - transmit)[None, :]], axis=0)


def composite(layers):
    while layers.shape[0] > 1:
        near_half = layers[0::2]
        far_half = layers[1::2]
        layers = near_half + (1.0 - near_half[:, 3:4]) * far_half
    return layers[0]


def body(bricks, colour_table, opacity_table, depth_order):
    palette = jnp.concatenate([colour_table, opacity_table[None, :]], axis=0)
    partial_value = render(bricks, palette)
    groups = lax.axis_size("grp")
    members = lax.axis_size("tile")
    pixels = partial_value.shape[1]
    sub_len = pixels // (groups * members)
    sectioned = partial_value.reshape(1, 4, groups, members, sub_len)
    layers = lax.all_to_all(sectioned, "tile", split_axis=3, concat_axis=0, tiled=True)
    layers = layers.reshape(members, 4, groups, sub_len)
    group_index = lax.axis_index("grp")
    rank_row = lax.dynamic_index_in_dim(depth_order, group_index, 0, keepdims=False)
    by_rank = jnp.argsort(rank_row)
    ordered = jnp.take(layers, by_rank, axis=0)
    own_group = composite(ordered)
    arrived = lax.all_to_all(own_group[None], "grp", split_axis=2, concat_axis=0, tiled=True)
    result = composite(arrived).reshape(4, sub_len)
    return result


def solution(mesh):
    in_specs = (P(("grp", "tile"), None, None), P(), P(), P())
    out_specs = P(None, ("grp", "tile"))
    return jax.shard_map(body, mesh=mesh, in_specs=in_specs, out_specs=out_specs, check_vma=False)
```

profile of v0, /device:TPU:8, one launch (start us, length us, event | category | flops | bytes accessed | tf_op | source)
XLA Modules:
  0.0 153.1 jit_solution(6230588998813952491)
XLA Ops:
  0.0 0.0 copy-start
  0.0 0.0 copy-start.2
  0.0 0.0 copy-start.1
  0.0 1.5 copy.10
  1.5 0.0 copy-done.2
  1.5 0.0 copy-done.1
  1.5 96.2 %while.16 = (s32[]{:T(128)}, f32[3,65536]{1,0:T(4,128)S(1)}, f32[65536]{0:T(1024)S(1)}, f32[2,65536]{1,0:T(2,128)S(1)}, f32[4,256]{1,0:T(4,128)S(1)}, /*index=5*...) while((s32[]{:T(128)}, f32[3,65536]{1,0:T(4,128)S(1)}, ...), condition=%wide.region_2.3_spmd.clone, body=%wide.region_1.2_spmd.clone.sunk | while | flops 873332736 | bytes 6062348 | solution.py:37
  1.8 0.6 dynamic-slice_multiply_fusion.9
  2.3 5.4 %fusion.147 = f32[4,65536]{1,0:T(4,128)S(1)} fusion(f32[4,256]{1,0:T(4,128)S(1)} %get-tuple-element.225, f32[8192]{0:T(1024)S(1)} %bitcast.147), kind=kOutput, calls=%fused_computation.16.clone.1 | convolution fusion | flops 109051904 | bytes 167936 | tf_op jit(solution)/shard_map/while/body/eval_jaxpr/dot_general | solution.py:12
  7.8 5.4 %fusion.148 = f32[4,65536]{1,0:T(4,128)S(1)} fusion(f32[4,65536]{1,0:T(4,128)S(1)} %fusion.147, f32[4,256]{1,0:T(4,128)S(1)} %get-tuple-element.225, f32[8192]{0:T(1024)S(1)} %bitcast.146), kind=kOutput, calls=%fused_computation.14.clone.1 | convolution fusion | flops 109051904 | bytes 167936 | tf_op jit(solution)/shard_map/while/body/eval_jaxpr/dot_general | solution.py:12
  13.2 6.0 %fusion.149 = f32[4,65536]{1,0:T(4,128)S(1)} fusion(f32[4,65536]{1,0:T(4,128)S(1)} %fusion.148, f32[4,256]{1,0:T(4,128)S(1)} %get-tuple-element.225, f32[8192]{0:T(1024)S(1)} %bitcast.145), kind=kOutput, calls=%fused_computation.12.clone.1 | convolution fusion | flops 109051904 | bytes 167936 | tf_op jit(solution)/shard_map/while/body/eval_jaxpr/dot_general | solution.py:12
  19.2 5.4 %fusion.150 = f32[4,65536]{1,0:T(4,128)S(1)} fusion(f32[4,65536]{1,0:T(4,128)S(1)} %fusion.149, f32[4,256]{1,0:T(4,128)S(1)} %get-tuple-element.225, f32[8192]{0:T(1024)S(1)} %bitcast.144), kind=kOutput, calls=%fused_computation.10.clone.1 | convolution fusion | flops 109051904 | bytes 167936 | tf_op jit(solution)/shard_map/while/body/eval_jaxpr/dot_general | solution.py:12
  24.6 5.6 %fusion.151 = f32[4,65536]{1,0:T(4,128)S(1)} fusion(f32[4,65536]{1,0:T(4,128)S(1)} %fusion.150, f32[4,256]{1,0:T(4,128)S(1)} %get-tuple-element.225, f32[8192]{0:T(1024)S(1)} %bitcast.143), kind=kOutput, calls=%fused_computation.8.clone.1 | convolution fusion | flops 109051904 | bytes 167936 | tf_op jit(solution)/shard_map/while/body/eval_jaxpr/dot_general | solution.py:12
  30.2 5.4 %fusion.152 = f32[4,65536]{1,0:T(4,128)S(1)} fusion(f32[4,65536]{1,0:T(4,128)S(1)} %fusion.151, f32[4,256]{1,0:T(4,128)S(1)} %get-tuple-element.225, f32[8192]{0:T(1024)S(1)} %bitcast.142), kind=kOutput, calls=%fused_computation.6.clone.1 | convolution fusion | flops 109051904 | bytes 167936 | tf_op jit(solution)/shard_map/while/body/eval_jaxpr/dot_general | solution.py:12
  35.7 5.7 %fusion.153 = f32[4,65536]{1,0:T(4,128)S(1)} fusion(f32[4,65536]{1,0:T(4,128)S(1)} %fusion.152, f32[4,256]{1,0:T(4,128)S(1)} %get-tuple-element.225, f32[8192]{0:T(1024)S(1)} %bitcast.141), kind=kOutput, calls=%fused_computation.4.clone.1 | convolution fusion | flops 109051904 | bytes 167936 | tf_op jit(solution)/shard_map/while/body/eval_jaxpr/dot_general | solution.py:12
  41.3 5.4 %fusion.154 = f32[4,65536]{1,0:T(4,128)S(1)} fusion(f32[4,65536]{1,0:T(4,128)S(1)} %fusion.153, f32[4,256]{1,0:T(4,128)S(1)} %get-tuple-element.225, f32[8192]{0:T(1024)S(1)} %bitcast.140), kind=kOutput, calls=%fused_computation.2.clone.1 | convolution fusion | flops 109051904 | bytes 167936 | tf_op jit(solution)/shard_map/while/body/eval_jaxpr/dot_general | solution.py:12
  46.8 0.3 slice.255
  47.1 0.2 subtract_multiply_fusion.2
  47.2 0.6 fusion.155
  48.3 0.6 dynamic-slice_multiply_fusion.9
  48.8 5.4 %fusion.147 = f32[4,65536]{1,0:T(4,128)S(1)} fusion(f32[4,256]{1,0:T(4,128)S(1)} %get-tuple-element.225, f32[8192]{0:T(1024)S(1)} %bitcast.147), kind=kOutput, calls=%fused_computation.16.clone.1 | convolution fusion | flops 109051904 | bytes 167936 | tf_op jit(solution)/shard_map/while/body/eval_jaxpr/dot_general | solution.py:12
  54.2 5.4 %fusion.148 = f32[4,65536]{1,0:T(4,128)S(1)} fusion(f32[4,65536]{1,0:T(4,128)S(1)} %fusion.147, f32[4,256]{1,0:T(4,128)S(1)} %get-tuple-element.225, f32[8192]{0:T(1024)S(1)} %bitcast.146), kind=kOutput, calls=%fused_computation.14.clone.1 | convolution fusion | flops 109051904 | bytes 167936 | tf_op jit(solution)/shard_map/while/body/eval_jaxpr/dot_general | solution.py:12
  59.7 5.6 %fusion.149 = f32[4,65536]{1,0:T(4,128)S(1)} fusion(f32[4,65536]{1,0:T(4,128)S(1)} %fusion.148, f32[4,256]{1,0:T(4,128)S(1)} %get-tuple-element.225, f32[8192]{0:T(1024)S(1)} %bitcast.145), kind=kOutput, calls=%fused_computation.12.clone.1 | convolution fusion | flops 109051904 | bytes 167936 | tf_op jit(solution)/shard_map/while/body/eval_jaxpr/dot_general | solution.py:12
  65.3 5.4 %fusion.150 = f32[4,65536]{1,0:T(4,128)S(1)} fusion(f32[4,65536]{1,0:T(4,128)S(1)} %fusion.149, f32[4,256]{1,0:T(4,128)S(1)} %get-tuple-element.225, f32[8192]{0:T(1024)S(1)} %bitcast.144), kind=kOutput, calls=%fused_computation.10.clone.1 | convolution fusion | flops 109051904 | bytes 167936 | tf_op jit(solution)/shard_map/while/body/eval_jaxpr/dot_general | solution.py:12
  70.8 5.7 %fusion.151 = f32[4,65536]{1,0:T(4,128)S(1)} fusion(f32[4,65536]{1,0:T(4,128)S(1)} %fusion.150, f32[4,256]{1,0:T(4,128)S(1)} %get-tuple-element.225, f32[8192]{0:T(1024)S(1)} %bitcast.143), kind=kOutput, calls=%fused_computation.8.clone.1 | convolution fusion | flops 109051904 | bytes 167936 | tf_op jit(solution)/shard_map/while/body/eval_jaxpr/dot_general | solution.py:12
  76.4 5.4 %fusion.152 = f32[4,65536]{1,0:T(4,128)S(1)} fusion(f32[4,65536]{1,0:T(4,128)S(1)} %fusion.151, f32[4,256]{1,0:T(4,128)S(1)} %get-tuple-element.225, f32[8192]{0:T(1024)S(1)} %bitcast.142), kind=kOutput, calls=%fused_computation.6.clone.1 | convolution fusion | flops 109051904 | bytes 167936 | tf_op jit(solution)/shard_map/while/body/eval_jaxpr/dot_general | solution.py:12
  81.9 5.8 %fusion.153 = f32[4,65536]{1,0:T(4,128)S(1)} fusion(f32[4,65536]{1,0:T(4,128)S(1)} %fusion.152, f32[4,256]{1,0:T(4,128)S(1)} %get-tuple-element.225, f32[8192]{0:T(1024)S(1)} %bitcast.141), kind=kOutput, calls=%fused_computation.4.clone.1 | convolution fusion | flops 109051904 | bytes 167936 | tf_op jit(solution)/shard_map/while/body/eval_jaxpr/dot_general | solution.py:12
  87.7 5.4 %fusion.154 = f32[4,65536]{1,0:T(4,128)S(1)} fusion(f32[4,65536]{1,0:T(4,128)S(1)} %fusion.153, f32[4,256]{1,0:T(4,128)S(1)} %get-tuple-element.225, f32[8192]{0:T(1024)S(1)} %bitcast.140), kind=kOutput, calls=%fused_computation.2.clone.1 | convolution fusion | flops 109051904 | bytes 167936 | tf_op jit(solution)/shard_map/while/body/eval_jaxpr/dot_general | solution.py:12
  93.1 0.3 slice.255
  93.4 0.2 subtract_multiply_fusion.2
  93.6 0.6 fusion.155
  97.8 0.1 concatenate.20
  97.8 0.2 copy.11
  98.0 0.1 pad_maximum_fusion
  98.1 1.7 %copy.7 = f32[1,4,4,64,256]{4,2,1,0,3:T(4,128)} copy(f32[1,4,4,64,256]{4,3,2,1,0:T(8,128)S(1)} %pad_maximum_fusion) | data formatting | bytes 2097152 | tf_op jit(solution)/shard_map/concatenate | solution.py:38
  99.7 12.1 %all-to-all-start = ((f32[1,4,4,64,256]{4,2,1,0,3:T(4,128)}), f32[1,4,4,64,256]{4,2,1,0,3:T(4,128)S(1)}, u32[]{:S(2)}, u32[]{:S(2)}) async-start(f32[1,4,4,64,256]{4,2,1,0,3:T(4,128)} %copy.7), calls=%async_computation | async-start | bytes 2097152 | tf_op jit(solution)/shard_map/all_to_all | solution.py:57
  111.9 0.0 copy-done
  111.9 2.0 %sort.17 = (s32[64]{0:T(128)}, s32[64]{0:T(128)S(1)}) sort(s32[64]{0:T(128)S(1)} %dynamic-slice_bitcast_fusion, s32[64]{0:T(128)S(1)} %iota.12), dimensions={0}, to_apply=%region_0.1 | sort | flops 384 | bytes 1024 | tf_op jit(solution)/shard_map/jit(argsort)/sort | solution.py:61
  114.0 26.7 %all-to-all-done = f32[1,4,4,64,256]{4,2,1,0,3:T(4,128)S(1)} async-done(((f32[1,4,4,64,256]{4,2,1,0,3:T(4,128)}), f32[1,4,4,64,256]{4,2,1,0,3:T(4,128)S(1)}, u32[]{:S(2)}, u32[]{:S(2)}) %all-to-all-start) | async-done | bytes 1048608 | tf_op jit(solution)/shard_map/all_to_all | solution.py:57
  140.6 1.2 gather_fusion
  141.8 0.3 broadcast_select_fusion
  142.2 0.2 multiply_add_fusion
  142.5 0.1 multiply_add_fusion.1
  142.8 9.5 %all_to_all.33 = f32[1,4,4,256]{3,1,0,2:T(4,128)S(1)} all-to-all(f32[1,4,4,256]{3,1,0,2:T(4,128)S(1)} %copy.8), channel_id=1, replica_groups=mesh['grp'=4,'tile'=64] {'grp'}, dimensions={2} | all-to-all | bytes 32768 | tf_op jit(solution)/shard_map/all_to_all | solution.py:64
  152.3 0.6 fusion.96
  (30 shorter events, 0.3 us)
Async XLA Ops:
  0.0 111.9 %copy-start = (s32[4,64]{1,0:T(4,128)S(1)}, s32[4,64]{1,0:T(4,128)}, u32[]{:S(2)}) copy-start(s32[4,64]{1,0:T(4,128)} %param.9) | copy-start | bytes 3076
  0.0 1.5 copy-start.2
  0.0 1.5 copy-start.1
  99.7 40.9 %all-to-all-start = ((f32[1,4,4,64,256]{4,2,1,0,3:T(4,128)}), f32[1,4,4,64,256]{4,2,1,0,3:T(4,128)S(1)}, u32[]{:S(2)}, u32[]{:S(2)}) async-start(f32[1,4,4,64,256]{4,2,1,0,3:T(4,128)} %copy.7), calls=%async_computation | async-start | bytes 2097152 | tf_op jit(solution)/shard_map/all_to_all | solution.py:57
where the time goes:
time: 155 us; the launch traced here: 153 us
  matrix products  88.8 us (57%)
  waiting for transfers between devices  26.7 us (17%)
  starting transfers between devices  12.1 us (8%)
  blocking collectives  9.46 us (6%)
  other arithmetic  6.19 us (4%)
  local copies, waits for them, and re-layouts  5.18 us (3%)
  loops' own time  4.23 us (3%)
    dot_general x16, matrix products, shade_cells(): jnp.dot(palette, weights, precision=lax.Precision.HIGHEST, preferred_elem...  88.8 us
    all_to_all x1, waiting for transfers between devices, body(): lax.all_to_all(sectioned, 'tile', split_axis=3, concat_axis=0, tiled=True)  26.7 us
    all_to_all x1, starting transfers between devices, body(): lax.all_to_all(sectioned, 'tile', split_axis=3, concat_axis=0, tiled=True)  12.1 us
    all_to_all x1, blocking collectives, body(): lax.all_to_all(own_group[None], 'grp', split_axis=2, concat_axis=0, tiled...  9.46 us
    another operation x1, loops' own time, render(): colour, transmit = lax.fori_loop(0, depth_count, one_slice, start)  4.23 us
  transfers between devices with their start and end apart: 1, of which 1 were waited for; matrix products, arithmetic and copies ran while one was open for 1% of the time, Pallas kernels for 0%

commit v1 on v0

--- a/solution.py
+++ b/solution.py
@@ -54,7 +54,12 @@
     pixels = partial_value.shape[1]
     sub_len = pixels // (groups * members)
     sectioned = partial_value.reshape(1, 4, groups, members, sub_len)
-    layers = lax.all_to_all(sectioned, "tile", split_axis=3, concat_axis=0, tiled=True)
+    layers = jnp.concatenate(
+        lax.all_to_all(
+            jnp.stack(jnp.split(sectioned, lax.axis_size("tile"), axis=3)), "tile", 0, 0
+        ),
+        axis=0,
+    )
     layers = layers.reshape(members, 4, groups, sub_len)
     group_index = lax.axis_index("grp")
     rank_row = lax.dynamic_index_in_dim(depth_order, group_index, 0, keepdims=False)

time: 155 us -> 156 us (level)
    concatenate x2, local copies, waits for them, and re-layouts: 1.74 us -> 0.09 us  [render(): return jnp.concatenate([colour, (1.0 - transmit)[None, :]], axis=0)]
where the time goes in v1:
time: 156 us; the launch traced here: 155 us
  matrix products  88.8 us (57%)
  waiting for transfers between devices  26.7 us (17%)
  starting transfers between devices  12.1 us (8%)
  blocking collectives  9.46 us (6%)
  local copies, waits for them, and re-layouts  6.28 us (4%)
  other arithmetic  6.12 us (4%)
  loops' own time  4.86 us (3%)
    dot_general x16, matrix products, shade_cells(): jnp.dot(palette, weights, precision=lax.Precision.HIGHEST, preferred_elem...  88.8 us
    all_to_all x1, waiting for transfers between devices, body(): lax.all_to_all(jnp.stack(jnp.split(sectioned, lax.axis_size('tile'), axis...  26.7 us
    all_to_all x1, starting transfers between devices, body(): lax.all_to_all(jnp.stack(jnp.split(sectioned, lax.axis_size('tile'), axis...  12.1 us
    all_to_all x1, blocking collectives, body(): lax.all_to_all(own_group[None], 'grp', split_axis=2, concat_axis=0, tiled...  9.46 us
    another operation x1, loops' own time, render(): colour, transmit = lax.fori_loop(0, depth_count, one_slice, start)  4.86 us
  transfers between devices with their start and end apart: 1, of which 1 were waited for; matrix products, arithmetic and copies ran while one was open for 1% of the time, Pallas kernels for 0%

profile of v1, /device:TPU:8, one launch (start us, length us, event | category | flops | bytes accessed | tf_op | source)
XLA Modules:
  0.0 155.0 jit_solution(2525341883476024231)
XLA Ops:
  0.0 0.0 copy-start
  0.0 0.0 copy-start.2
  0.0 0.0 copy-start.1
  0.0 1.5 copy.136
  1.5 0.0 copy-done.2
  1.5 0.0 copy-done.1
  1.5 96.8 %while.16 = (s32[]{:T(128)}, f32[3,65536]{1,0:T(4,128)S(1)}, f32[65536]{0:T(1024)S(1)}, f32[2,65536]{1,0:T(2,128)S(1)}, f32[4,256]{1,0:T(4,128)S(1)}, /*index=5*...) while((s32[]{:T(128)}, f32[3,65536]{1,0:T(4,128)S(1)}, ...), condition=%wide.region_2.3_spmd.clone, body=%wide.region_1.2_spmd.clone.sunk | while | flops 873332736 | bytes 6062340 | solution.py:37
  1.8 0.6 dynamic-slice_multiply_fusion.9
  2.3 5.4 %fusion.147 = f32[4,65536]{1,0:T(4,128)S(1)} fusion(f32[4,256]{1,0:T(4,128)S(1)} %get-tuple-element.225, f32[8192]{0:T(1024)S(1)} %bitcast.399), kind=kOutput, calls=%fused_computation.16.clone.1 | convolution fusion | flops 109051904 | bytes 167936 | tf_op jit(solution)/shard_map/while/body/eval_jaxpr/dot_general | solution.py:12
  7.8 5.4 %fusion.148 = f32[4,65536]{1,0:T(4,128)S(1)} fusion(f32[4,65536]{1,0:T(4,128)S(1)} %fusion.147, f32[4,256]{1,0:T(4,128)S(1)} %get-tuple-element.225, f32[8192]{0:T(1024)S(1)} %bitcast.398), kind=kOutput, calls=%fused_computation.14.clone.1 | convolution fusion | flops 109051904 | bytes 167936 | tf_op jit(solution)/shard_map/while/body/eval_jaxpr/dot_general | solution.py:12
  13.2 6.0 %fusion.149 = f32[4,65536]{1,0:T(4,128)S(1)} fusion(f32[4,65536]{1,0:T(4,128)S(1)} %fusion.148, f32[4,256]{1,0:T(4,128)S(1)} %get-tuple-element.225, f32[8192]{0:T(1024)S(1)} %bitcast.397), kind=kOutput, calls=%fused_computation.12.clone.1 | convolution fusion | flops 109051904 | bytes 167936 | tf_op jit(solution)/shard_map/while/body/eval_jaxpr/dot_general | solution.py:12
  19.2 5.4 %fusion.150 = f32[4,65536]{1,0:T(4,128)S(1)} fusion(f32[4,65536]{1,0:T(4,128)S(1)} %fusion.149, f32[4,256]{1,0:T(4,128)S(1)} %get-tuple-element.225, f32[8192]{0:T(1024)S(1)} %bitcast.396), kind=kOutput, calls=%fused_computation.10.clone.1 | convolution fusion | flops 109051904 | bytes 167936 | tf_op jit(solution)/shard_map/while/body/eval_jaxpr/dot_general | solution.py:12
  24.6 5.6 %fusion.151 = f32[4,65536]{1,0:T(4,128)S(1)} fusion(f32[4,65536]{1,0:T(4,128)S(1)} %fusion.150, f32[4,256]{1,0:T(4,128)S(1)} %get-tuple-element.225, f32[8192]{0:T(1024)S(1)} %bitcast.395), kind=kOutput, calls=%fused_computation.8.clone.1 | convolution fusion | flops 109051904 | bytes 167936 | tf_op jit(solution)/shard_map/while/body/eval_jaxpr/dot_general | solution.py:12
  30.2 5.4 %fusion.152 = f32[4,65536]{1,0:T(4,128)S(1)} fusion(f32[4,65536]{1,0:T(4,128)S(1)} %fusion.151, f32[4,256]{1,0:T(4,128)S(1)} %get-tuple-element.225, f32[8192]{0:T(1024)S(1)} %bitcast.394), kind=kOutput, calls=%fused_computation.6.clone.1 | convolution fusion | flops 109051904 | bytes 167936 | tf_op jit(solution)/shard_map/while/body/eval_jaxpr/dot_general | solution.py:12
  35.7 5.7 %fusion.153 = f32[4,65536]{1,0:T(4,128)S(1)} fusion(f32[4,65536]{1,0:T(4,128)S(1)} %fusion.152, f32[4,256]{1,0:T(4,128)S(1)} %get-tuple-element.225, f32[8192]{0:T(1024)S(1)} %bitcast.393), kind=kOutput, calls=%fused_computation.4.clone.1 | convolution fusion | flops 109051904 | bytes 167936 | tf_op jit(solution)/shard_map/while/body/eval_jaxpr/dot_general | solution.py:12
  41.3 5.4 %fusion.154 = f32[4,65536]{1,0:T(4,128)S(1)} fusion(f32[4,65536]{1,0:T(4,128)S(1)} %fusion.153, f32[4,256]{1,0:T(4,128)S(1)} %get-tuple-element.225, f32[8192]{0:T(1024)S(1)} %bitcast.392), kind=kOutput, calls=%fused_computation.2.clone.1 | convolution fusion | flops 109051904 | bytes 167936 | tf_op jit(solution)/shard_map/while/body/eval_jaxpr/dot_general | solution.py:12
  46.8 0.3 slice.255
  47.1 0.2 subtract_multiply_fusion.2
  47.2 0.6 fusion.155
  48.3 0.6 dynamic-slice_multiply_fusion.9
  48.8 5.4 %fusion.147 = f32[4,65536]{1,0:T(4,128)S(1)} fusion(f32[4,256]{1,0:T(4,128)S(1)} %get-tuple-element.225, f32[8192]{0:T(1024)S(1)} %bitcast.399), kind=kOutput, calls=%fused_computation.16.clone.1 | convolution fusion | flops 109051904 | bytes 167936 | tf_op jit(solution)/shard_map/while/body/eval_jaxpr/dot_general | solution.py:12
  54.2 5.4 %fusion.148 = f32[4,65536]{1,0:T(4,128)S(1)} fusion(f32[4,65536]{1,0:T(4,128)S(1)} %fusion.147, f32[4,256]{1,0:T(4,128)S(1)} %get-tuple-element.225, f32[8192]{0:T(1024)S(1)} %bitcast.398), kind=kOutput, calls=%fused_computation.14.clone.1 | convolution fusion | flops 109051904 | bytes 167936 | tf_op jit(solution)/shard_map/while/body/eval_jaxpr/dot_general | solution.py:12
  59.7 5.6 %fusion.149 = f32[4,65536]{1,0:T(4,128)S(1)} fusion(f32[4,65536]{1,0:T(4,128)S(1)} %fusion.148, f32[4,256]{1,0:T(4,128)S(1)} %get-tuple-element.225, f32[8192]{0:T(1024)S(1)} %bitcast.397), kind=kOutput, calls=%fused_computation.12.clone.1 | convolution fusion | flops 109051904 | bytes 167936 | tf_op jit(solution)/shard_map/while/body/eval_jaxpr/dot_general | solution.py:12
  65.3 5.4 %fusion.150 = f32[4,65536]{1,0:T(4,128)S(1)} fusion(f32[4,65536]{1,0:T(4,128)S(1)} %fusion.149, f32[4,256]{1,0:T(4,128)S(1)} %get-tuple-element.225, f32[8192]{0:T(1024)S(1)} %bitcast.396), kind=kOutput, calls=%fused_computation.10.clone.1 | convolution fusion | flops 109051904 | bytes 167936 | tf_op jit(solution)/shard_map/while/body/eval_jaxpr/dot_general | solution.py:12
  70.8 5.7 %fusion.151 = f32[4,65536]{1,0:T(4,128)S(1)} fusion(f32[4,65536]{1,0:T(4,128)S(1)} %fusion.150, f32[4,256]{1,0:T(4,128)S(1)} %get-tuple-element.225, f32[8192]{0:T(1024)S(1)} %bitcast.395), kind=kOutput, calls=%fused_computation.8.clone.1 | convolution fusion | flops 109051904 | bytes 167936 | tf_op jit(solution)/shard_map/while/body/eval_jaxpr/dot_general | solution.py:12
  76.4 5.4 %fusion.152 = f32[4,65536]{1,0:T(4,128)S(1)} fusion(f32[4,65536]{1,0:T(4,128)S(1)} %fusion.151, f32[4,256]{1,0:T(4,128)S(1)} %get-tuple-element.225, f32[8192]{0:T(1024)S(1)} %bitcast.394), kind=kOutput, calls=%fused_computation.6.clone.1 | convolution fusion | flops 109051904 | bytes 167936 | tf_op jit(solution)/shard_map/while/body/eval_jaxpr/dot_general | solution.py:12
  81.9 5.8 %fusion.153 = f32[4,65536]{1,0:T(4,128)S(1)} fusion(f32[4,65536]{1,0:T(4,128)S(1)} %fusion.152, f32[4,256]{1,0:T(4,128)S(1)} %get-tuple-element.225, f32[8192]{0:T(1024)S(1)} %bitcast.393), kind=kOutput, calls=%fused_computation.4.clone.1 | convolution fusion | flops 109051904 | bytes 167936 | tf_op jit(solution)/shard_map/while/body/eval_jaxpr/dot_general | solution.py:12
  87.7 5.4 %fusion.154 = f32[4,65536]{1,0:T(4,128)S(1)} fusion(f32[4,65536]{1,0:T(4,128)S(1)} %fusion.153, f32[4,256]{1,0:T(4,128)S(1)} %get-tuple-element.225, f32[8192]{0:T(1024)S(1)} %bitcast.392), kind=kOutput, calls=%fused_computation.2.clone.1 | convolution fusion | flops 109051904 | bytes 167936 | tf_op jit(solution)/shard_map/while/body/eval_jaxpr/dot_general | solution.py:12
  93.1 0.3 slice.255
  93.4 0.2 subtract_multiply_fusion.2
  93.6 0.6 fusion.155
  98.4 0.2 copy.137
  98.5 0.1 constant_dynamic-update-slice_fusion.1
  98.6 0.1 concatenate.20
  100.4 1.3 copy.133
  101.6 12.1 %all-to-all-start = ((f32[64,1,4,4,1,256]{5,3,2,4,1,0:T(4,128)}), f32[64,1,4,4,1,256]{5,3,2,4,1,0:T(4,128)S(1)}, u32[]{:S(2)}, u32[]{:S(2)}) async-start(f32[64,1,4,4,1,256]{5,3,2,4,1,0:T(4,128)} %copy.133), calls=%async_computation | async-start | bytes 2097152 | tf_op jit(solution)/shard_map/all_to_all | solution.py:58
  113.8 0.0 copy-done
  113.8 2.0 %sort.17 = (s32[64]{0:T(128)}, s32[64]{0:T(128)S(1)}) sort(s32[64]{0:T(128)S(1)} %dynamic-slice_bitcast_fusion, s32[64]{0:T(128)S(1)} %iota.12), dimensions={0}, to_apply=%region_0.1 | sort | flops 384 | bytes 1024 | tf_op jit(solution)/shard_map/jit(argsort)/sort | solution.py:66
  115.9 26.7 %all-to-all-done = f32[64,1,4,4,1,256]{5,3,2,4,1,0:T(4,128)S(1)} async-done(((f32[64,1,4,4,1,256]{5,3,2,4,1,0:T(4,128)}), f32[64,1,4,4,1,256]{5,3,2,4,1,0:T(4,128)S(1)}, u32[]{:S(2)}, u32[]{:S(2)}) %all-to-all-start) | async-done | bytes 1048608 | tf_op jit(solution)/shard_map/all_to_all | solution.py:58
  142.5 1.2 gather_fusion
  143.7 0.3 broadcast_select_fusion
  144.1 0.2 multiply_add_fusion
  144.4 0.1 multiply_add_fusion.1
  144.7 9.5 %all_to_all.23 = f32[1,4,4,256]{3,1,0,2:T(4,128)S(1)} all-to-all(f32[1,4,4,256]{3,1,0,2:T(4,128)S(1)} %copy.134), channel_id=1, replica_groups=mesh['grp'=4,'tile'=64] {'grp'}, dimensions={2} | all-to-all | bytes 32768 | tf_op jit(solution)/shard_map/all_to_all | solution.py:69
  154.2 0.6 fusion.96
  (95 shorter events, 1.8 us)
Async XLA Ops:
  0.0 113.8 %copy-start = (s32[4,64]{1,0:T(4,128)S(1)}, s32[4,64]{1,0:T(4,128)}, u32[]{:S(2)}) copy-start(s32[4,64]{1,0:T(4,128)} %param.9) | copy-start | bytes 3076
  0.0 1.5 copy-start.2
  0.0 1.5 copy-start.1
  101.6 40.9 %all-to-all-start = ((f32[64,1,4,4,1,256]{5,3,2,4,1,0:T(4,128)}), f32[64,1,4,4,1,256]{5,3,2,4,1,0:T(4,128)S(1)}, u32[]{:S(2)}, u32[]{:S(2)}) async-start(f32[64,1,4,4,1,256]{5,3,2,4,1,0:T(4,128)} %copy.133), calls=%async_computation | async-start | bytes 2097152 | tf_op jit(solution)/shard_map/all_to_all | solution.py:58
